TPU v7x, 512 devices: a whole 4x8x8 slice. The times are simulated.
512 devices in a mesh: tm: 8 (over x, z_hi), vert: 64 (over y, z_lo, core).
Axes of the slice: x: 4, y: 8, z: 8 (z_hi: 2, z_lo: 4; z = z_hi * 4 + z_lo), core: 2. Of those that a mesh axis runs over, the one named last changes fastest.
Arguments:
- frames: bfloat16 [16, 8192, 256], P('tm', 'vert'), may hold values from -12 to 12
- cotangent: bfloat16 [16, 8192, 256], P('tm', 'vert'), may hold values from -200 to 200
- table: int32 [8192, 7], P('vert'), may hold values from -1 to 8191, as said below
- w_conv: bfloat16 [1792, 256], replicated, may hold values from -0.125 to 0.125
- w_attn: bfloat16 [4, 256, 256], replicated, may hold values from -0.375 to 0.375
Outputs:
- grad_frames: bfloat16 [16, 8192, 256], P('tm', 'vert')
- grad_conv: bfloat16 [1792, 256], replicated
- grad_attn: bfloat16 [4, 256, 256], replicated
Inputs may be any that keep to these rules, and one draw needn't show every extreme that they name: `table`: each entry of row v is -1 (an empty slot) or a vertex at most 64 places from v in the vertex order; slot 0 is v itself; some entries lie exactly 64 places away on either side.
All inputs are finite; a program needn't handle non-finite values.
Results may differ from a plain program's by a relative error of at most 0.014.
The roundings to bfloat16 on the way count: a program that leaves them out, or rounds other values in their place, can miss the bound.
Values may be sent and summed in bfloat16 or wider, within the bound.
No kernel may reach another device: no remote copies, remote signals or barrier semaphores. Data moves between devices by JAX's collectives and lax.ppermute only.
A program may use at most 64 MiB of HBM per device.

v0:
```python
import math
import jax
import jax.numpy as jnp
from jax import lax
from jax.sharding import PartitionSpec as P

TF = 16
HEADS = 8
HW = 64


def extended_2(block, sides, width):
    for axis, dim in sides:
        count = lax.axis_size(axis)
        forward = [(i, i + 1) for i in range(count - 1)]
        backward = [(target, source) for source, target in forward]
        low = lax.ppermute(
            lax.slice_in_dim(block, block.shape[dim] - width, None, axis=dim), axis, forward
        )
        high = lax.ppermute(lax.slice_in_dim(block, 0, width, axis=dim), axis, backward)
        block = jnp.concatenate([low, block, high], axis=dim)
    return block


def cross_rows(left, right):
    return lax.dot_general(
        left, right, (((0,), (0,)), ((), ())), preferred_element_type=jnp.float32
    )


def project(rows, weight):
    return jnp.dot(rows, weight, preferred_element_type=jnp.float32).astype(jnp.bfloat16)


def frame_attention(query_rows, key_rows, value_rows, grad_out):
    frames_q, verts, width = query_rows.shape
    head_dim = width // HEADS
    scaling = head_dim ** (-0.5)
    query_heads = query_rows.reshape(frames_q, verts, HEADS, head_dim)
    key_heads = key_rows.reshape(-1, verts, HEADS, head_dim)
    value_heads = value_rows.reshape(-1, verts, HEADS, head_dim)
    grad_heads = grad_out.reshape(frames_q, verts, HEADS, head_dim)
    scores = (
        jnp.einsum("frhd,grhd->rhfg", query_heads, key_heads, preferred_element_type=jnp.float32)
        * scaling
    )
    top_score = jnp.max(scores, axis=-1, keepdims=True)
    expo = jnp.exp(scores - top_score)
    probs = expo / jnp.sum(expo, axis=-1, keepdims=True)
    probs_b = probs.astype(jnp.bfloat16)
    attended = jnp.einsum(
        "rhfg,grhd->frhd", probs_b, value_heads, preferred_element_type=jnp.float32
    ).astype(jnp.bfloat16)
    grad_value = jnp.einsum(
        "rhfg,frhd->grhd", probs_b, grad_heads, preferred_element_type=jnp.float32
    ).astype(jnp.bfloat16)
    grad_probs = jnp.einsum(
        "frhd,grhd->rhfg", grad_heads, value_heads, preferred_element_type=jnp.float32
    )
    inner_sum = jnp.sum(probs * grad_probs, axis=-1, keepdims=True)
    grad_scores = (scaling * probs * (grad_probs - inner_sum)).astype(jnp.bfloat16)
    grad_query = jnp.einsum(
        "rhfg,grhd->frhd", grad_scores, key_heads, preferred_element_type=jnp.float32
    ).astype(jnp.bfloat16)
    grad_key = jnp.einsum(
        "rhfg,frhd->grhd", grad_scores, query_heads, preferred_element_type=jnp.float32
    ).astype(jnp.bfloat16)
    return (
        attended.reshape(frames_q, verts, width),
        grad_query.reshape(frames_q, verts, width),
        grad_key.reshape(-1, verts, width),
        grad_value.reshape(-1, verts, width),
    )


def body(frames, cotangent, table, w_conv, w_attn):
    local_frames, patch, width = frames.shape
    stencil = table.shape[1]
    start = lax.axis_index("vert") * patch
    extended = extended_2(frames, (("vert", 1),), HW)
    padded = jnp.concatenate([extended, jnp.zeros((local_frames, 1, width), jnp.bfloat16)], axis=1)
    blank_row = patch + 2 * HW
    local_index = jnp.where(table < 0, blank_row, table - start + HW).reshape(-1)
    gathered = jnp.take(padded, local_index, axis=1).reshape(local_frames * patch, stencil * width)
    conv_pre = jnp.dot(gathered, w_conv, preferred_element_type=jnp.float32)
    gate_sig = jax.nn.sigmoid(conv_pre)
    hidden = (frames.reshape(-1, width).astype(jnp.float32) + conv_pre * gate_sig).astype(
        jnp.bfloat16
    )
    hidden_time, grad_time = (
        lax.all_to_all(
            hidden.reshape(local_frames, patch, width),
            "tm",
            split_axis=1,
            concat_axis=0,
            tiled=True,
        ),
        lax.all_to_all(cotangent, "tm", split_axis=1, concat_axis=0, tiled=True),
    )
    shape3 = hidden_time.shape
    rows_time = hidden_time.reshape(-1, width)
    grad_rows = grad_time.reshape(-1, width)
    query_rows = project(rows_time, w_attn[0])
    key_rows = project(rows_time, w_attn[1])
    value_rows = project(rows_time, w_attn[2])
    grad_out = project(grad_rows, w_attn[3].T)
    attended, grad_query, grad_key, grad_value = frame_attention(
        query_rows.reshape(shape3),
        key_rows.reshape(shape3),
        value_rows.reshape(shape3),
        grad_out.reshape(shape3),
    )
    grad_wout = cross_rows(attended.reshape(-1, width), grad_rows)
    grad_query = grad_query.reshape(-1, width)
    grad_key = grad_key.reshape(-1, width)
    grad_value = grad_value.reshape(-1, width)
    grad_hidden = (
        grad_rows.astype(jnp.float32)
        + jnp.dot(grad_query, w_attn[0].T, preferred_element_type=jnp.float32)
        + jnp.dot(grad_key, w_attn[1].T, preferred_element_type=jnp.float32)
        + jnp.dot(grad_value, w_attn[2].T, preferred_element_type=jnp.float32)
    ).astype(jnp.bfloat16)
    weight_parts = [
        cross_rows(rows_time, grad_query),
        cross_rows(rows_time, grad_key),
        cross_rows(rows_time, grad_value),
    ]
    back_hidden = lax.all_to_all(
        grad_hidden.reshape(shape3), "tm", split_axis=0, concat_axis=1, tiled=True
    )
    grad_attn = jnp.stack(weight_parts + [grad_wout])
    back_rows = back_hidden.reshape(-1, width)
    grad_pre = (
        back_rows.astype(jnp.float32) * gate_sig * (1.0 + conv_pre * (1.0 - gate_sig))
    ).astype(jnp.bfloat16)
    grad_conv = cross_rows(gathered, grad_pre)
    grad_gathered = lax.dot_general(
        grad_pre, w_conv, (((1,), (1,)), ((), ())), preferred_element_type=jnp.float32
    )
    grad_ext = (
        jnp.zeros((local_frames, blank_row + 1, width), jnp.float32)
        .at[:, local_index]
        .add(grad_gathered.reshape(local_frames, patch * stencil, width))
    )
    rim = jnp.concatenate([grad_ext[:, :HW], grad_ext[:, patch + HW : patch + 2 * HW]], axis=1)
    arrived = extended_2(rim, (("vert", 1),), HW)
    grad_local = grad_ext[:, HW : HW + patch]
    grad_local = grad_local.at[:, :HW].add(arrived[:, :HW])
    grad_local = grad_local.at[:, patch - HW :].add(arrived[:, 3 * HW :])
    grad_frames = (back_hidden.astype(jnp.float32) + grad_local).astype(jnp.bfloat16)
    grad_conv, grad_attn = lax.psum((grad_conv, grad_attn), ("tm", "vert"))
    scaling = 1.0 / math.sqrt(TF * patch * lax.axis_size("vert"))
    return (
        grad_frames,
        (grad_conv * scaling).astype(jnp.bfloat16),
        (grad_attn * scaling).astype(jnp.bfloat16),
    )


def solution(mesh):
    return jax.shard_map(
        body,
        mesh=mesh,
        in_specs=(P("tm", "vert", None), P("tm", "vert", None), P("vert", None), P(), P()),
        out_specs=(P("tm", "vert", None), P(), P()),
        check_vma=False,
    )
```

profile of v0, /device:TPU:24, one launch (start us, length us, event | category | flops | bytes accessed | tf_op | source)
XLA Modules:
  0.0 392.5 jit_solution(10169680832873045731)
XLA Ops:
  7.2 1.1 copy.75
  8.4 1.9 collective-permute-start
  10.3 7.2 %collective-permute-start.1 = (bf16[2,64,256]{2,0,1:T(2,128)(2,1)S(1)}, bf16[2,64,256]{2,0,1:T(2,128)(2,1)S(1)}, u32[]{:S(2)}, u32[]{:S(2)}) collective-permute-start(bf16[2,64,256]{2,0,1:T(2,128)(2,1)S(1)} %get-tuple-element.44), channel_id=1, source_target_pairs={{1,0},{2,1},{3,2},{4,3},{5,4},{6,5},{7,6},{8,7},{9,8},{10,9},{11,1... | collective-permute-start | bytes 196616 | tf_op jit(solution)/shard_map/ppermute | solution.py:20
  17.6 1.7 copy.72
  19.3 11.9 %all-to-all-start = ((bf16[2,128,256]{2,0,1:T(2,128)(2,1)}), bf16[2,128,256]{2,0,1:T(2,128)(2,1)S(1)}, u32[]{:S(2)}, u32[]{:S(2)}) async-start(bf16[2,128,256]{2,0,1:T(2,128)(2,1)} %copy.72), calls=%async_computation | async-start | bytes 262144 | tf_op jit(solution)/shard_map/all_to_all | solution.py:98
  31.1 0.7 add_select_fusion
  32.4 0.5 maximum_maximum_fusion
  32.9 4.5 %gather_fusion = bf16[896,2,256]{2,1,0:T(2,128)(2,1)S(1)} fusion(bf16[2,257,256]{2,0,1:T(2,128)(2,1)S(1)} %maximum_maximum_fusion, s32[1024]{0:T(1024)S(1)} %pad_clamp_fusion), kind=kCustom, calls=%fused_computation | custom fusion | bytes 1838592 | tf_op jit(solution)/shard_map/jit(_take)/gather | solution.py:84
  37.4 3.3 fusion.8
  40.9 0.9 select_n.33
  41.8 1.1 fusion.18
  42.9 0.8 copy.80
  43.7 9.6 %all-to-all-start.1 = ((bf16[2,128,256]{2,0,1:T(2,128)(2,1)}), bf16[2,128,256]{2,0,1:T(2,128)(2,1)S(1)}, u32[]{:S(2)}, u32[]{:S(2)}) async-start(bf16[2,128,256]{2,0,1:T(2,128)(2,1)} %copy.80), calls=%async_computation.1 | async-start | bytes 262144 | tf_op jit(solution)/shard_map/all_to_all | solution.py:91
  53.6 1.0 reshape_reshape.26
  54.6 9.3 %all-to-all-done.1 = bf16[2,128,256]{2,0,1:T(2,128)(2,1)S(1)} async-done(((bf16[2,128,256]{2,0,1:T(2,128)(2,1)}), bf16[2,128,256]{2,0,1:T(2,128)(2,1)S(1)}, u32[]{:S(2)}, u32[]{:S(2)}) %all-to-all-start.1) | async-done | bytes 131104 | tf_op jit(solution)/shard_map/all_to_all | solution.py:91
  65.0 1.0 reshape_reshape.27
  66.1 2.0 fusion.53
  68.1 2.5 multiply_reduce_fusion
  70.9 1.3 fusion.5
  72.2 0.5 fusion.3
  72.7 1.3 fusion.6
  74.0 1.3 fusion.4
  75.5 0.4 reshape_reshape.28
  75.8 0.9 convolution_bitcast_fusion.3
  76.7 1.8 convolution_add_fusion.2
  79.1 0.9 convolution_bitcast_fusion.2
  80.0 1.2 copy.93
  81.3 0.4 reshape_reshape.30
  81.6 0.9 convolution_bitcast_fusion.1
  82.5 1.2 copy.99
  84.1 1.2 convolution_add_fusion.1
  85.3 0.9 fusion.7
  86.2 3.4 all-to-all-start.2
  89.9 2.1 pad_maximum_fusion
  92.0 8.1 %all-to-all-done.2 = bf16[16,16,256]{2,1,0:T(8,128)(2,1)S(1)} async-done(((bf16[16,16,256]{2,1,0:T(8,128)(2,1)}), bf16[16,16,256]{2,1,0:T(8,128)(2,1)S(1)}, u32[]{:S(2)}, u32[]{:S(2)}) %all-to-all-start.2) | async-done | bytes 131104 | tf_op jit(solution)/shard_map/all_to_all | solution.py:128
  100.3 1.7 fusion.59
  102.0 1.7 fusion.58
  103.7 1.6 reshape.164
  105.3 2.7 copy.136
  108.1 62.6 %scatter_fusion = f32[2,257,256]{2,0,1:T(2,128)S(1)} fusion(f32[2,257,256]{2,0,1:T(2,128)S(1)} %broadcast_in_dim.28, s32[896]{0:T(1024)S(1)} %fusion.40, f32[896,2,256]{2,1,0:T(2,128)} %bitcast.98), kind=kCustom, calls=%fused_computation.1 | custom fusion | flops 458752 | bytes 5508608 | tf_op jit(solution)/shard_map/scatter-add | solution.py:143
  170.8 1.9 collective-permute-start.2
  172.9 6.3 %collective-permute-start.3 = (f32[2,64,256]{2,0,1:T(2,128)S(1)}, f32[2,64,256]{2,0,1:T(2,128)S(1)}, u32[]{:S(2)}, u32[]{:S(2)}) collective-permute-start(f32[2,64,256]{2,0,1:T(2,128)S(1)} %get-tuple-element.41), channel_id=1, source_target_pairs={{1,0},{2,1},{3,2},{4,3},{5,4},{6,5},{7,6},{8,7},{9,8},{10,9},{11,1... | collective-permute-start | bytes 393224 | tf_op jit(solution)/shard_map/ppermute | solution.py:20
  179.3 0.6 collective-permute-done.2
  180.0 1.8 collective-permute-done.3
  182.1 0.7 copy.100
  182.8 199.3 %all-reduce.3.cloned.1.call-done = (f32[1792,256]{1,0:T(8,128)}, f32[4,256,256]{2,1,0:T(8,128)}) async-done(((f32[1792,256]{1,0:T(8,128)}, f32[4,256,256]{2,1,0:T(8,128)}), (f32[1792,256]{1,0:T(8,128)}, f32[4,256,256]{2,1,0:T(8,128)})) %all-reduce.3.cloned.1.call-update) | async-done | bytes 2883600 | tf_op jit(solution)/shard_map/psum | solution.py:151
  382.1 2.7 multiply_convert_fusion
  384.8 0.9 multiply_convert_fusion.1
  (61 shorter events, 4.6 us)
Async XLA Ops:
  7.2 34.6 %copy-start = (bf16[1792,256]{1,0:T(8,128)(2,1)S(1)}, bf16[1792,256]{1,0:T(8,128)(2,1)}, u32[]{:S(2)}) copy-start(bf16[1792,256]{1,0:T(8,128)(2,1)} %param.12) | copy-start | bytes 2752516
  8.4 24.0 %collective-permute-start = (bf16[2,64,256]{2,0,1:T(2,128)(2,1)S(1)}, bf16[2,64,256]{2,0,1:T(2,128)(2,1)S(1)}, u32[]{:S(2)}, u32[]{:S(2)}) collective-permute-start(bf16[2,64,256]{2,0,1:T(2,128)(2,1)S(1)} %get-tuple-element.43), channel_id=1, source_target_pairs={{0,1},{1,2},{2,3},{3,4},{4,5},{5,6},{6,7},{7,8},{8,9},{9,10},{10,1... | collective-permute-start | bytes 196616 | tf_op jit(solution)/shard_map/ppermute | solution.py:17
  10.3 22.1 %collective-permute-start.1 = (bf16[2,64,256]{2,0,1:T(2,128)(2,1)S(1)}, bf16[2,64,256]{2,0,1:T(2,128)(2,1)S(1)}, u32[]{:S(2)}, u32[]{:S(2)}) collective-permute-start(bf16[2,64,256]{2,0,1:T(2,128)(2,1)S(1)} %get-tuple-element.44), channel_id=1, source_target_pairs={{1,0},{2,1},{3,2},{4,3},{5,4},{6,5},{7,6},{8,7},{9,8},{10,9},{11,1... | collective-permute-start | bytes 196616 | tf_op jit(solution)/shard_map/ppermute | solution.py:20
  19.3 24.5 %all-to-all-start = ((bf16[2,128,256]{2,0,1:T(2,128)(2,1)}), bf16[2,128,256]{2,0,1:T(2,128)(2,1)S(1)}, u32[]{:S(2)}, u32[]{:S(2)}) async-start(bf16[2,128,256]{2,0,1:T(2,128)(2,1)} %copy.72), calls=%async_computation | async-start | bytes 262144 | tf_op jit(solution)/shard_map/all_to_all | solution.py:98
  40.7 1.0 copy-start.10
  41.8 11.6 %copy-start.2 = (bf16[4,256,256]{2,1,0:T(8,128)(2,1)S(1)}, bf16[4,256,256]{2,1,0:T(8,128)(2,1)}, u32[]{:S(2)}) copy-start(bf16[4,256,256]{2,1,0:T(8,128)(2,1)} %param.13) | copy-start | bytes 1572868
  43.7 20.2 %all-to-all-start.1 = ((bf16[2,128,256]{2,0,1:T(2,128)(2,1)}), bf16[2,128,256]{2,0,1:T(2,128)(2,1)S(1)}, u32[]{:S(2)}, u32[]{:S(2)}) async-start(bf16[2,128,256]{2,0,1:T(2,128)(2,1)} %copy.80), calls=%async_computation.1 | async-start | bytes 262144 | tf_op jit(solution)/shard_map/all_to_all | solution.py:91
  68.0 2.5 copy-start.5
  70.9 1.8 copy-start.7
  72.6 1.4 copy-start.8
  75.3 3.3 copy-start.1
  80.0 4.1 %copy-start.3 = (bf16[4,256,256]{2,1,0:T(8,128)(2,1)S(1)}, bf16[4,256,256]{2,1,0:T(8,128)(2,1)}, u32[]{:S(2)}) copy-start(bf16[4,256,256]{2,1,0:T(8,128)(2,1)} %param.13) | copy-start | bytes 1572868
  84.1 5.8 %copy-start.6 = (f32[1,256,256]{2,1,0:T(8,128)S(1)}, f32[1,256,256]{2,1,0:T(8,128)}, u32[]{:S(2)}) copy-start(f32[1,256,256]{2,1,0:T(8,128)} %convolution_bitcast_fusion.1) | copy-start | bytes 786436
  86.2 13.9 %all-to-all-start.2 = ((bf16[16,16,256]{2,1,0:T(8,128)(2,1)}), bf16[16,16,256]{2,1,0:T(8,128)(2,1)S(1)}, u32[]{:S(2)}, u32[]{:S(2)}) async-start(bf16[16,16,256]{2,1,0:T(8,128)(2,1)} %bitcast.17), calls=%async_computation.2 | async-start | bytes 262144 | tf_op jit(solution)/shard_map/all_to_all | solution.py:128
  89.6 10.6 %copy-start.9 = (f32[256,256]{1,0:T(8,128)S(1)}, f32[256,256]{1,0:T(8,128)}, u32[]{:S(2)}) copy-start(f32[256,256]{1,0:T(8,128)} %get-tuple-element.46) | copy-start | bytes 786436
  89.6 292.5 %all-reduce.3.cloned.1.call-start = ((), (), s32[]{:S(2)}) async-start(), calls=%async_computation.3 | async-start | bytes 5767168 | tf_op jit(solution)/shard_map/psum | solution.py:151
  170.8 9.2 %collective-permute-start.2 = (f32[2,64,256]{2,0,1:T(2,128)S(1)}, f32[2,64,256]{2,0,1:T(2,128)S(1)}, u32[]{:S(2)}, u32[]{:S(2)}) collective-permute-start(f32[2,64,256]{2,0,1:T(2,128)S(1)} %get-tuple-element.42), channel_id=1, source_target_pairs={{0,1},{1,2},{2,3},{3,4},{4,5},{5,6},{6,7},{7,8},{8,9},{9,10},{10,1... | collective-permute-start | bytes 393224 | tf_op jit(solution)/shard_map/ppermute | solution.py:17
  172.9 8.8 %collective-permute-start.3 = (f32[2,64,256]{2,0,1:T(2,128)S(1)}, f32[2,64,256]{2,0,1:T(2,128)S(1)}, u32[]{:S(2)}, u32[]{:S(2)}) collective-permute-start(f32[2,64,256]{2,0,1:T(2,128)S(1)} %get-tuple-element.41), channel_id=1, source_target_pairs={{1,0},{2,1},{3,2},{4,3},{5,4},{6,5},{7,6},{8,7},{9,8},{10,9},{11,1... | collective-permute-start | bytes 393224 | tf_op jit(solution)/shard_map/ppermute | solution.py:20
  382.1 2.7 copy-start.4
Sparse Core Ops, SparseCore 0:
  102.1 279.8 all-reduce.2
where the time goes:
time: 397 us; the launch traced here: 393 us
  waiting for transfers between devices  219 us (55%)
  other arithmetic  73.7 us (19%)
  starting transfers between devices  42.3 us (11%)
  local copies, waits for them, and re-layouts  21.8 us (5%)
  matrix products  21.1 us (5%)
  between operations  14.5 us (4%)
    psum x1, waiting for transfers between devices, body(): grad_conv, grad_attn = lax.psum((grad_conv, grad_attn), ('tm', 'vert'))  199 us
    scatter-add x1, other arithmetic, body(): grad_ext = jnp.zeros((local_frames, blank_row + 1, width), jnp.float32).a...  62.6 us
    ppermute x2, starting transfers between devices, extended_2(): lax.ppermute(lax.slice_in_dim(block, 0, width, axis=dim), axis, backward)  13.6 us
    all_to_all x1, starting transfers between devices, body(): lax.all_to_all(cotangent, 'tm', split_axis=1, concat_axis=0, tiled=True)  11.9 us
    all_to_all x1, starting transfers between devices, body(): lax.all_to_all(hidden.reshape(local_frames, patch, width), 'tm', split_ax...  9.61 us
    all_to_all x1, waiting for transfers between devices, body(): lax.all_to_all(hidden.reshape(local_frames, patch, width), 'tm', split_ax...  9.32 us
    all_to_all x1, waiting for transfers between devices, body(): lax.all_to_all(grad_hidden.reshape(shape3), 'tm', split_axis=0, concat_ax...  8.14 us
  transfers between devices with their start and end apart: 8, of which 5 were waited for; matrix products, arithmetic and copies ran while one was open for 22% of the time, Pallas kernels for 0%

commit v1 on v0

--- a/solution.py
+++ b/solution.py
@@ -148,7 +148,13 @@
     grad_local = grad_local.at[:, :HW].add(arrived[:, :HW])
     grad_local = grad_local.at[:, patch - HW :].add(arrived[:, 3 * HW :])
     grad_frames = (back_hidden.astype(jnp.float32) + grad_local).astype(jnp.bfloat16)
-    grad_conv, grad_attn = lax.psum((grad_conv, grad_attn), ("tm", "vert"))
+
+    def detail_the_pieces_all(packet):
+        for w in ("vert", "tm"):
+            packet = jax.lax.psum(packet, w)
+        return packet
+
+    grad_conv, grad_attn = detail_the_pieces_all((grad_conv, grad_attn))
     scaling = 1.0 / math.sqrt(TF * patch * lax.axis_size("vert"))
     return (
         grad_frames,

time: 397 us -> 925 us (2.33)
  the two profiles are of different devices: /device:TPU:24 before, /device:TPU:1 now
where the time goes in v1:
time: 925 us; the launch traced here: 920 us
  waiting for transfers between devices  751 us (81%)
  other arithmetic  73.6 us (8%)
  starting transfers between devices  38.2 us (4%)
  local copies, waits for them, and re-layouts  21.8 us (2%)
  matrix products  21.1 us (2%)
  between operations  14.5 us (2%)
    psum x2, waiting for transfers between devices, detail_the_pieces_all(): packet = jax.lax.psum(packet, w)  728 us
    scatter-add x1, other arithmetic, body(): grad_ext = jnp.zeros((local_frames, blank_row + 1, width), jnp.float32).a...  62.6 us
  transfers between devices with their start and end apart: 9, of which 6 were waited for; matrix products, arithmetic and copies ran while one was open for 10% of the time, Pallas kernels for 0%

profile of v1, /device:TPU:1, one launch (start us, length us, event | category | flops | bytes accessed | tf_op | source)
XLA Modules:
  0.0 920.0 jit_solution(1976495826019323786)
XLA Ops:
  7.2 1.1 copy.75
  8.4 5.4 collective-permute-start
  13.8 4.7 collective-permute-start.1
  18.5 1.7 copy.72
  20.2 8.8 all-to-all-start
  29.0 0.7 add_select_fusion
  30.3 0.5 maximum_maximum_fusion
  30.7 4.5 gather_fusion
  35.3 3.3 fusion.8
  38.7 0.9 select_n.33
  39.6 1.1 fusion.18
  40.8 0.8 copy.80
  41.6 9.1 all-to-all-start.1
  50.9 1.0 reshape_reshape.26
  51.9 8.3 all-to-all-done.1
  61.4 1.0 reshape_reshape.27
  62.4 2.0 fusion.53
  64.4 2.5 multiply_reduce_fusion
  67.2 1.3 fusion.5
  68.5 0.5 fusion.3
  69.0 1.3 fusion.6
  70.3 1.3 fusion.4
  71.8 0.4 reshape_reshape.28
  72.1 0.9 convolution_bitcast_fusion.3
  73.1 1.8 convolution_add_fusion.2
  75.4 0.9 convolution_bitcast_fusion.2
  76.3 1.2 copy.93
  77.9 0.9 convolution_bitcast_fusion.1
  78.9 1.2 copy.99
  80.4 1.2 convolution_add_fusion.1
  81.6 0.9 fusion.7
  82.5 3.4 all-to-all-start.2
  86.2 2.1 pad_maximum_fusion
  88.3 7.5 all-to-all-done.2
  95.9 1.7 fusion.59
  97.7 546.0 %all-reduce.5.cloned.1.call-done = (f32[1792,256]{1,0:T(8,128)}, f32[4,256,256]{2,1,0:T(8,128)}) async-done(((f32[1792,256]{1,0:T(8,128)}, f32[4,256,256]{2,1,0:T(8,128)}), (f32[1792,256]{1,0:T(8,128)}, f32[4,256,256]{2,1,0:T(8,128)})) %all-reduce.5.cloned.1.call-update) | async-done | bytes 2883600 | tf_op jit(solution)/shard_map/psum | solution.py:154
  643.8 1.7 fusion.58
  645.5 1.6 reshape.164
  647.0 2.7 copy.136
  649.9 62.6 %scatter_fusion = f32[2,257,256]{2,0,1:T(2,128)S(1)} fusion(f32[2,257,256]{2,0,1:T(2,128)S(1)} %broadcast_in_dim.28, s32[896]{0:T(1024)S(1)} %fusion.40, f32[896,2,256]{2,1,0:T(2,128)} %bitcast.98), kind=kCustom, calls=%fused_computation.1 | custom fusion | flops 458752 | bytes 5508608 | tf_op jit(solution)/shard_map/scatter-add | solution.py:143
  712.5 3.3 collective-permute-start.2
  716.0 3.6 collective-permute-start.3
  719.6 1.4 collective-permute-done.2
  721.1 5.5 collective-permute-done.3
  726.9 0.7 copy.100
  727.6 182.0 %all-reduce.7.cloned.1.call-done = (f32[1792,256]{1,0:T(8,128)}, f32[4,256,256]{2,1,0:T(8,128)}) async-done(((f32[1792,256]{1,0:T(8,128)}, f32[4,256,256]{2,1,0:T(8,128)}), (f32[1792,256]{1,0:T(8,128)}, f32[4,256,256]{2,1,0:T(8,128)})) %all-reduce.7.cloned.1.call-update) | async-done | bytes 2883600 | tf_op jit(solution)/shard_map/psum | solution.py:154
  909.6 2.7 multiply_convert_fusion
  912.3 0.9 multiply_convert_fusion.1
  (64 shorter events, 5.0 us)
Async XLA Ops:
  7.2 32.5 %copy-start = (bf16[1792,256]{1,0:T(8,128)(2,1)S(1)}, bf16[1792,256]{1,0:T(8,128)(2,1)}, u32[]{:S(2)}) copy-start(bf16[1792,256]{1,0:T(8,128)(2,1)} %param.12) | copy-start | bytes 2752516
  8.4 21.9 %collective-permute-start = (bf16[2,64,256]{2,0,1:T(2,128)(2,1)S(1)}, bf16[2,64,256]{2,0,1:T(2,128)(2,1)S(1)}, u32[]{:S(2)}, u32[]{:S(2)}) collective-permute-start(bf16[2,64,256]{2,0,1:T(2,128)(2,1)S(1)} %get-tuple-element.45), channel_id=1, source_target_pairs={{0,1},{1,2},{2,3},{3,4},{4,5},{5,6},{6,7},{7,8},{8,9},{9,10},{10,1... | collective-permute-start | bytes 196616 | tf_op jit(solution)/shard_map/ppermute | solution.py:17
  13.8 16.5 %collective-permute-start.1 = (bf16[2,64,256]{2,0,1:T(2,128)(2,1)S(1)}, bf16[2,64,256]{2,0,1:T(2,128)(2,1)S(1)}, u32[]{:S(2)}, u32[]{:S(2)}) collective-permute-start(bf16[2,64,256]{2,0,1:T(2,128)(2,1)S(1)} %get-tuple-element.46), channel_id=1, source_target_pairs={{1,0},{2,1},{3,2},{4,3},{5,4},{6,5},{7,6},{8,7},{9,8},{10,9},{11,1... | collective-permute-start | bytes 196616 | tf_op jit(solution)/shard_map/ppermute | solution.py:20
  20.2 21.4 %all-to-all-start = ((bf16[2,128,256]{2,0,1:T(2,128)(2,1)}), bf16[2,128,256]{2,0,1:T(2,128)(2,1)S(1)}, u32[]{:S(2)}, u32[]{:S(2)}) async-start(bf16[2,128,256]{2,0,1:T(2,128)(2,1)} %copy.72), calls=%async_computation | async-start | bytes 262144 | tf_op jit(solution)/shard_map/all_to_all | solution.py:98
  38.6 1.0 copy-start.10
  39.6 11.0 %copy-start.2 = (bf16[4,256,256]{2,1,0:T(8,128)(2,1)S(1)}, bf16[4,256,256]{2,1,0:T(8,128)(2,1)}, u32[]{:S(2)}) copy-start(bf16[4,256,256]{2,1,0:T(8,128)(2,1)} %param.13) | copy-start | bytes 1572868
  41.6 18.7 %all-to-all-start.1 = ((bf16[2,128,256]{2,0,1:T(2,128)(2,1)}), bf16[2,128,256]{2,0,1:T(2,128)(2,1)S(1)}, u32[]{:S(2)}, u32[]{:S(2)}) async-start(bf16[2,128,256]{2,0,1:T(2,128)(2,1)} %copy.80), calls=%async_computation.1 | async-start | bytes 262144 | tf_op jit(solution)/shard_map/all_to_all | solution.py:91
  64.4 2.5 copy-start.5
  67.2 1.8 copy-start.7
  69.0 1.4 copy-start.8
  71.6 3.3 copy-start.1
  76.3 4.1 copy-start.3
  80.4 5.8 copy-start.6
  82.5 13.2 %all-to-all-start.2 = ((bf16[16,16,256]{2,1,0:T(8,128)(2,1)}), bf16[16,16,256]{2,1,0:T(8,128)(2,1)S(1)}, u32[]{:S(2)}, u32[]{:S(2)}) async-start(bf16[16,16,256]{2,1,0:T(8,128)(2,1)} %bitcast.17), calls=%async_computation.2 | async-start | bytes 262144 | tf_op jit(solution)/shard_map/all_to_all | solution.py:128
  85.9 9.9 %copy-start.9 = (f32[256,256]{1,0:T(8,128)S(1)}, f32[256,256]{1,0:T(8,128)}, u32[]{:S(2)}) copy-start(f32[256,256]{1,0:T(8,128)} %get-tuple-element.48) | copy-start | bytes 786436
  85.9 557.8 %all-reduce.5.cloned.1.call-start = ((), (), s32[]{:S(2)}) async-start(), calls=%async_computation.3 | async-start | bytes 5767168 | tf_op jit(solution)/shard_map/psum | solution.py:154
  97.7 811.9 %all-reduce.7.cloned.1.call-start = ((), (), s32[]{:S(2)}) async-start(), calls=%async_computation.4 | async-start | bytes 5767168 | tf_op jit(solution)/shard_map/psum | solution.py:154
  712.5 8.5 collective-permute-start.2
  716.0 10.6 %collective-permute-start.3 = (f32[2,64,256]{2,0,1:T(2,128)S(1)}, f32[2,64,256]{2,0,1:T(2,128)S(1)}, u32[]{:S(2)}, u32[]{:S(2)}) collective-permute-start(f32[2,64,256]{2,0,1:T(2,128)S(1)} %get-tuple-element.43), channel_id=1, source_target_pairs={{1,0},{2,1},{3,2},{4,3},{5,4},{6,5},{7,6},{8,7},{9,8},{10,9},{11,1... | collective-permute-start | bytes 393224 | tf_op jit(solution)/shard_map/ppermute | solution.py:20
  909.6 2.7 copy-start.4
Sparse Core Ops, SparseCore 0:
  97.8 545.9 all-reduce.4
  646.8 262.7 all-reduce.6
